TPU v7x, 32 devices: a whole 2x2x4 slice. The times are simulated.
32 devices in a mesh: freq: 4 (over z), tm: 4 (over x, core), grp: 2 (over y).
Axes of the slice: x: 2, y: 2, z: 4, core: 2. Of those that a mesh axis runs over, the one named last changes fastest.
Arguments:
- voltages: bfloat16 [4, 2, 1024, 4096], P(None, None, ('freq', 'grp'), 'tm'), may hold values from -6 to 6
- prior_gains: float32 [4, 2, 1024], P('freq'), may hold values from -4.2 to 4.2
- station_flags: int32 [512], replicated, may hold values 0 or 1
- ingest_map: int32 [512], replicated, may hold values from 0 to 511, each once
- station_coords: float32 [2, 512], replicated, may hold values from -40 to 40
- pointing: int32 [2, 256], replicated, may hold values from 0 to 63
- corr_channels: int32 [4], replicated, may hold values from 0 to 3, each once
- beam_channels: int32 [4], replicated, may hold values from 0 to 3, each once
Outputs:
- visibilities: float32 [4, 2, 1024, 1024], P('freq', None, 'grp', 'tm')
- solved_gains: float32 [4, 2, 1024], P('freq')
- tied_beams: bfloat16 [4, 2, 2, 256, 4096], P('freq', None, None, 'grp', 'tm')
Inputs may be any that keep to these rules, and one draw needn't show every extreme that they name: `ingest_map`: each station appears in exactly one ingest slot. `corr_channels`: each channel is handled by exactly one correlator slot. `beam_channels`: each channel is handled by exactly one beamformer slot.
All inputs are finite; a program needn't handle non-finite values.
Results may differ from a plain program's by a relative error of at most 0.0049.
Values may be sent and summed in bfloat16 or wider, within the bound.
A program may use at most 64 MiB of HBM per device.

v0:
```python
import math
import jax
import jax.numpy as jnp
from jax import lax
from jax.sharding import PartitionSpec as P

S = 512
ITERS = 4
grid_cells = 64.0


def weights_for(gains_sel, ratio, pointing_part, slot_coords):
    east_dir = (pointing_part[0].astype(jnp.float32) + 0.5) / grid_cells - 0.5
    north_dir = (pointing_part[1].astype(jnp.float32) + 0.5) / grid_cells - 0.5
    phase = (
        2.0
        * math.pi
        * ratio
        * (
            east_dir[:, None] * slot_coords[0][None, :]
            + north_dir[:, None] * slot_coords[1][None, :]
        )
    )
    cosine = jnp.cos(phase)
    sine = jnp.sin(phase)
    gain_real = gains_sel[0].reshape(2, S)
    gain_imag = gains_sel[1].reshape(2, S)
    denom = jnp.maximum(gain_real * gain_real + gain_imag * gain_imag, 0.5)
    along_real = gain_real / denom
    along_imag = gain_imag / denom
    factor = 1.0 / math.sqrt(S)
    w_real = (cosine[None] * along_real[:, None, :] - sine[None] * along_imag[:, None, :]) * factor
    w_imag = -(cosine[None] * along_imag[:, None, :] + sine[None] * along_real[:, None, :]) * factor
    upper = jnp.stack([w_real, -w_imag], axis=2)
    lower = jnp.stack([w_imag, w_real], axis=2)
    return jnp.stack([upper, lower], axis=1).astype(jnp.bfloat16)


def body(
    voltages,
    prior_gains,
    station_flags,
    ingest_map,
    station_coords,
    pointing,
    corr_channels,
    beam_channels,
):
    highest = lax.Precision.HIGHEST
    n_freq = lax.axis_size("freq")
    n_time = lax.axis_size("tm")
    n_group = lax.axis_size("grp")
    freq_index = lax.axis_index("freq")
    time_index = lax.axis_index("tm")
    group_index = lax.axis_index("grp")
    channels_all = voltages.shape[0]
    per_device = channels_all // n_freq
    per_input = voltages.shape[2]
    samples = voltages.shape[3]
    inputs_all = 2 * S
    corr_source = jnp.take(voltages, corr_channels, axis=0)
    beam_source = jnp.take(voltages, beam_channels, axis=0)
    corr_half, beam_half = (
        lax.all_to_all(corr_source, "freq", split_axis=0, concat_axis=2, tiled=True),
        lax.all_to_all(beam_source, "freq", split_axis=0, concat_axis=2, tiled=True),
    )
    split_shape = (per_device, 2, n_freq, per_input, samples)
    corr_pair, beam_pair = (
        lax.all_gather(corr_half.reshape(split_shape), "grp", axis=3, tiled=True),
        lax.all_gather(beam_half.reshape(split_shape), "grp", axis=3, tiled=True),
    )
    full_shape = (per_device, 2, inputs_all, samples)
    corr_volts = corr_pair.reshape(full_shape)
    beam_volts = beam_pair.reshape(full_shape)
    slot_keep = 1 - jnp.take(station_flags, ingest_map)
    keep = jnp.concatenate([slot_keep, slot_keep]).astype(jnp.bfloat16)
    corr_volts = corr_volts * keep[None, None, :, None]
    beam_volts = beam_volts * keep[None, None, :, None]
    rows = inputs_all // n_group
    row_start = group_index * rows
    mine = lax.dynamic_slice_in_dim(corr_volts, row_start, rows, 2)
    left = jnp.stack([mine, jnp.stack([mine[:, 1], -mine[:, 0]], axis=1)], axis=1)
    partial_value = jnp.einsum(
        "corit,crjt->coij", left, corr_volts, preferred_element_type=jnp.float32
    )
    partial_value = partial_value * (1.0 / (samples * n_time))
    columns = inputs_all // n_time
    vis_block = lax.psum_scatter(partial_value, "tm", scatter_dimension=3, tiled=True)
    gains = prior_gains
    for iteration in range(ITERS):
        power = jnp.sum(gains * gains, axis=(1, 2)) + 1e-06
        along = lax.dynamic_slice_in_dim(gains, time_index * columns, columns, 2)
        real_real = jnp.einsum("cij,cj->ci", vis_block[:, 0], along[:, 0], precision=highest)
        imag_imag = jnp.einsum("cij,cj->ci", vis_block[:, 1], along[:, 1], precision=highest)
        real_imag = jnp.einsum("cij,cj->ci", vis_block[:, 0], along[:, 1], precision=highest)
        imag_real = jnp.einsum("cij,cj->ci", vis_block[:, 1], along[:, 0], precision=highest)
        update = jnp.stack([real_real - imag_imag, imag_real + real_imag], axis=1)
        update = lax.psum(update, "tm")
        own_rows = lax.dynamic_slice_in_dim(gains, row_start, rows, 2)
        fresh = 0.5 * (own_rows + inputs_all * update / power[:, None, None])
        gains = lax.all_gather(fresh, "grp", axis=2, tiled=True)
    all_gains = lax.all_gather(gains, "freq", axis=0, tiled=True)
    my_beam = lax.dynamic_slice_in_dim(beam_channels, freq_index * per_device, per_device, 0)
    onehot = (corr_channels[None, :] == my_beam[:, None]).astype(jnp.float32)
    selected = jnp.einsum("ck,kri->cri", onehot, all_gains, precision=highest)
    ratio = 0.875 + 0.25 * (my_beam.astype(jnp.float32) + 0.5) / channels_all
    beams_mine = pointing.shape[1] // n_group
    pointing_part = lax.dynamic_slice_in_dim(pointing, group_index * beams_mine, beams_mine, 1)
    slot_coords = jnp.take(station_coords, ingest_map, axis=1)
    weights = jax.vmap(weights_for, in_axes=(0, 0, None, None))(
        selected, ratio, pointing_part, slot_coords
    )
    block = beam_volts.reshape(per_device, 2, 2, S, samples)
    beams = jnp.einsum("cpobrq,crpqt->cpobt", weights, block, preferred_element_type=jnp.float32)
    return (vis_block, gains, beams.astype(jnp.bfloat16))


def solution(mesh):
    return jax.shard_map(
        body,
        mesh=mesh,
        in_specs=(
            P(None, None, ("freq", "grp"), "tm"),
            P("freq", None, None),
            P(),
            P(),
            P(),
            P(),
            P(),
            P(),
        ),
        out_specs=(
            P("freq", None, "grp", "tm"),
            P("freq", None, None),
            P("freq", None, None, "grp", "tm"),
        ),
        check_vma=False,
    )
```

profile of v0, /device:TPU:0, one launch (start us, length us, event | category | flops | bytes accessed | tf_op | source)
XLA Modules:
  0.0 313.8 jit_solution(3851320219780948037)
XLA Ops:
  7.2 0.8 compare_select_fusion.1
  8.0 0.7 compare_and_fusion
  8.8 2.0 gather_fusion.2
  10.8 1.9 broadcast_select_fusion.1
  12.7 54.4 %all_to_all.30 = bf16[4,2,128,1024]{3,2,1,0:T(8,128)(2,1)} all-to-all(bf16[4,2,128,1024]{3,2,1,0:T(8,128)(2,1)S(1)} %broadcast_select_fusion.1), channel_id=1, replica_groups=mesh['freq'=4,'tm'=4,'grp'=2] {'freq'}, dimensions={0} | all-to-all | bytes 4194304 | tf_op jit(solution)/shard_map/all_to_all | solution.py:64
  67.2 2.0 gather_fusion.3
  69.2 1.9 broadcast_select_fusion
  71.1 50.7 %all_to_all.31 = bf16[4,2,128,1024]{3,2,1,0:T(8,128)(2,1)} all-to-all(bf16[4,2,128,1024]{3,2,1,0:T(8,128)(2,1)S(1)} %broadcast_select_fusion), channel_id=1, replica_groups=mesh['freq'=4,'tm'=4,'grp'=2] {'freq'}, dimensions={0} | all-to-all | bytes 4194304 | tf_op jit(solution)/shard_map/all_to_all | solution.py:65
  121.8 0.6 copy-done.5
  122.5 3.5 %gather_fusion = s32[512]{0:T(512)S(1)} fusion(s32[512]{0:T(512)S(1)} %copy-done.1, s32[1024]{0:T(1024)S(1)} %pad_clamp_fusion.1), kind=kCustom, calls=%fused_computation.2 | custom fusion | bytes 6144 | tf_op jit(solution)/shard_map/jit(_take)/gather | solution.py:75
  126.1 2.5 broadcast_multiply_fusion
  129.1 1.8 copy-done.3
  132.6 6.1 %fusion.5 = f32[1,2,512,1024]{3,2,1,0:T(8,128)} fusion(bf16[2,1024,1024,1]{2,1,0,3:T(8,128)(2,1)S(1)} %bitcast.171, bf16[1,1,2,512,1024]{4,3,2,1,0:T(8,128)(2,1)S(1)} %maximum_bitcast_fusion.4, bf16[1,1,2,512,1024]{4,3,2,1,0:T(8,128)(2,1)S(1)} %fusion.76), kind=kOutput, calls=%fused_computation.11 | convolution fusion | flops 4298113024 | bytes 12582912 | tf_op jit(solution)/shard_map/corit,crjt->coij/dot_general | solution.py:83
  138.8 0.6 copy-done.8
  139.4 0.6 dynamic_slice.42
  140.1 1.0 gather_fusion.1
  141.8 0.6 multiply_reduce_fusion.3
  143.5 1.8 fusion.32
  145.3 36.2 %all-gather.5.cloned.1.call-done = bf16[1,2,4,256,1024]{4,3,1,2,0:T(8,128)(2,1)} async-done(((bf16[1,2,4,128,1024]{4,3,1,2,0:T(8,128)(2,1)}), bf16[1,2,4,256,1024]{4,3,1,2,0:T(8,128)(2,1)}) %all-gather.5.cloned.1.call-update) | async-done | bytes 4194320 | tf_op jit(solution)/shard_map/all_gather | solution.py:70
  181.6 4.6 %copy.27 = bf16[1,2,4,256,1024]{4,3,2,1,0:T(8,128)(2,1)} copy(bf16[1,2,4,256,1024]{4,3,1,2,0:T(8,128)(2,1)} %all-gather.5.cloned.1.call-done) | data formatting | bytes 8388608 | tf_op jit(solution)/shard_map/all_gather | solution.py:70
  186.2 42.9 %reduce-scatter.2.cloned.1.call-done = f32[1,2,512,256]{3,2,1,0:T(8,128)} async-done(((f32[1,2,512,1024]{3,2,1,0:T(8,128)}), f32[1,2,512,256]{3,2,1,0:T(8,128)}) %reduce-scatter.2.cloned.1.call-update) | async-done | bytes 1048592 | tf_op jit(solution)/shard_map/reduce_scatter | solution.py:88
  229.1 1.7 fusion.29
  230.8 1.6 fusion.21
  232.4 1.6 fusion.22
  234.0 1.6 fusion.30
  235.6 5.8 %psum.28 = f32[1,2,512]{2,1,0:T(2,128)S(1)} all-reduce(f32[1,2,512]{2,1,0:T(2,128)S(1)} %pad_maximum_fusion), channel_id=1, replica_groups=mesh['freq'=4,'tm'=4,'grp'=2] {'tm'}, use_global_device_ids=true, to_apply=%region_1.3 | all-reduce | flops 1024 | bytes 8192 | tf_op jit(solution)/shard_map/psum | solution.py:98
  241.4 4.4 %all_gather.22 = f32[1,2,1024]{2,1,0:T(2,128)S(1)} all-gather(f32[1,2,512]{2,1,0:T(2,128)S(1)} %fusion.38), channel_id=1, replica_groups=mesh['freq'=4,'tm'=4,'grp'=2] {'grp'}, dimensions={2}, use_global_device_ids=true | all-gather | bytes 12288 | tf_op jit(solution)/shard_map/all_gather | solution.py:101
  245.8 0.6 multiply_reduce_fusion.2
  246.9 0.6 fusion.19
  247.5 0.6 fusion.20
  248.0 0.6 fusion.28
  248.6 5.7 %psum.29 = f32[1,2,512]{2,1,0:T(2,128)S(1)} all-reduce(f32[1,2,512]{2,1,0:T(2,128)S(1)} %pad_maximum_fusion.1), channel_id=1, replica_groups=mesh['freq'=4,'tm'=4,'grp'=2] {'tm'}, use_global_device_ids=true, to_apply=%region_3.5 | all-reduce | flops 1024 | bytes 8192 | tf_op jit(solution)/shard_map/psum | solution.py:98
  255.0 4.5 %all_gather.23 = f32[1,2,1024]{2,1,0:T(2,128)S(1)} all-gather(f32[1,2,512]{2,1,0:T(2,128)S(1)} %fusion.39), channel_id=1, replica_groups=mesh['freq'=4,'tm'=4,'grp'=2] {'grp'}, dimensions={2}, use_global_device_ids=true | all-gather | bytes 12288 | tf_op jit(solution)/shard_map/all_gather | solution.py:101
  259.5 0.6 multiply_reduce_fusion.1
  260.6 0.6 fusion.17
  261.8 0.6 fusion.26
  262.4 5.7 %psum.30 = f32[1,2,512]{2,1,0:T(2,128)S(1)} all-reduce(f32[1,2,512]{2,1,0:T(2,128)S(1)} %pad_maximum_fusion.2), channel_id=1, replica_groups=mesh['freq'=4,'tm'=4,'grp'=2] {'tm'}, use_global_device_ids=true, to_apply=%region_5.7 | all-reduce | flops 1024 | bytes 8192 | tf_op jit(solution)/shard_map/psum | solution.py:98
  268.7 4.4 %all_gather.24 = f32[1,2,1024]{2,1,0:T(2,128)S(1)} all-gather(f32[1,2,512]{2,1,0:T(2,128)S(1)} %fusion.40), channel_id=1, replica_groups=mesh['freq'=4,'tm'=4,'grp'=2] {'grp'}, dimensions={2}, use_global_device_ids=true | all-gather | bytes 12288 | tf_op jit(solution)/shard_map/all_gather | solution.py:101
  273.1 0.6 multiply_reduce_fusion
  274.2 0.6 fusion.15
  275.3 0.6 fusion.24
  275.9 5.7 %psum.31 = f32[1,2,512]{2,1,0:T(2,128)S(1)} all-reduce(f32[1,2,512]{2,1,0:T(2,128)S(1)} %pad_maximum_fusion.3), channel_id=1, replica_groups=mesh['freq'=4,'tm'=4,'grp'=2] {'tm'}, use_global_device_ids=true, to_apply=%region_7.9 | all-reduce | flops 1024 | bytes 8192 | tf_op jit(solution)/shard_map/psum | solution.py:98
  282.3 4.4 %all_gather.25 = f32[1,2,1024]{2,1,0:T(2,128)S(1)} all-gather(f32[1,2,512]{2,1,0:T(2,128)S(1)} %fusion.41), channel_id=1, replica_groups=mesh['freq'=4,'tm'=4,'grp'=2] {'grp'}, dimensions={2}, use_global_device_ids=true | all-gather | bytes 12288 | tf_op jit(solution)/shard_map/all_gather | solution.py:101
  286.6 13.4 %all_gather.26 = f32[4,2,1024]{2,1,0:T(2,128)S(1)} all-gather(f32[1,2,1024]{2,1,0:T(2,128)S(1)} %all_gather.25), channel_id=1, replica_groups=mesh['freq'=4,'tm'=4,'grp'=2] {'freq'}, dimensions={0}, use_global_device_ids=true | all-gather | bytes 40960 | tf_op jit(solution)/shard_map/all_gather | solution.py:102
  300.0 0.8 fusion.33
  300.9 1.1 negate_convert_fusion
  302.1 4.6 %fusion.8 = bf16[1,2,2,128,1024]{4,3,2,1,0:T(8,128)(2,1)} fusion(bf16[2,1,128,2,512]{4,2,3,1,0:T(8,128)(2,1)S(1)} %get-tuple-element.17, bf16[2,1,128,2,512]{4,2,3,1,0:T(8,128)(2,1)S(1)} %get-tuple-element.16, bf16[2,2,512,1024]{3,2,1,0:T(8,128)(2,1)} %bitcast.170, bf16[2,512]{1,0:T(2,128)(2,1)S(1)} %convert_element_type.50), kind=kOutput, calls=%fused_computation.19 | convolution fusion | flops 1076887552 | bytes 6293504 | tf_op jit(solution)/shard_map/cpobrq,crpqt->cpobt/dot_general | solution.py:114
  306.6 0.6 copy.47
  (71 shorter events, 6.1 us)
Async XLA Ops:
  7.2 1.6 copy-start
  7.2 118.9 %all-gather.3.cloned.1.call-start = ((), (), s32[]{:S(2)}) async-start(), calls=%async_computation.3 | async-start | bytes 6291456 | tf_op jit(solution)/shard_map/all_gather | solution.py:69
  67.2 114.4 %all-gather.5.cloned.1.call-start = ((), (), s32[]{:S(2)}) async-start(), calls=%async_computation.5 | async-start | bytes 6291456 | tf_op jit(solution)/shard_map/all_gather | solution.py:70
  121.8 0.7 copy-start.5
  121.8 0.7 copy-start.1
  121.8 107.3 %reduce-scatter.2.cloned.1.call-start = ((), (), s32[]{:S(2)}) async-start(), calls=%async_computation.4 | async-start | bytes 5242880 | tf_op jit(solution)/shard_map/reduce_scatter | solution.py:88
  128.7 2.3 copy-start.3
  138.7 0.7 copy-start.8
  138.7 1.3 copy-start.7
  138.7 3.1 copy-start.4
  138.7 4.3 %copy-start.9 = (s32[2,256]{1,0:T(2,128)S(1)}, s32[2,256]{1,0:T(2,128)}, u32[]{:S(2)}) copy-start(s32[2,256]{1,0:T(2,128)} %param.15) | copy-start | bytes 6148
  229.1 17.3 %copy-start.2 = (f32[1,2,512,256]{3,2,1,0:T(8,128)S(1)}, f32[1,2,512,256]{3,2,1,0:T(8,128)}, u32[]{:S(2)}) copy-start(f32[1,2,512,256]{3,2,1,0:T(8,128)} %reduce-scatter.2.cloned.1.call-done) | copy-start | bytes 3145732
  260.1 39.9 %copy-start.6 = (s32[4]{0:T(128)S(1)}, s32[4]{0:T(128)}, u32[]{:S(2)}) copy-start(s32[4]{0:T(128)} %param.16) | copy-start | bytes 52
Sparse Core Ops, SparseCore 0:
  67.3 55.9 all-gather.2
  124.8 56.7 all-gather.4
  184.7 44.3 reduce-scatter.1
where the time goes:
time: 315 us; the launch traced here: 314 us
  blocking collectives  159 us (50%)
  waiting for transfers between devices  79.2 us (25%)
  matrix products  24.5 us (8%)
  local copies, waits for them, and re-layouts  19 us (6%)
  between operations  17.3 us (5%)
  other arithmetic  14.7 us (5%)
    all_to_all x1, blocking collectives, body(): lax.all_to_all(corr_source, 'freq', split_axis=0, concat_axis=2, tiled=True)  54.4 us
    all_to_all x1, blocking collectives, body(): lax.all_to_all(beam_source, 'freq', split_axis=0, concat_axis=2, tiled=True)  50.7 us
    reduce_scatter x1, waiting for transfers between devices, body(): lax.psum_scatter(partial_value, 'tm', scatter_dimension=3, tiled=True)  42.9 us
    all_gather x1, waiting for transfers between devices, body(): lax.all_gather(beam_half.reshape(split_shape), 'grp', axis=3, tiled=True)  36.2 us
    psum x4, blocking collectives, body(): update = lax.psum(update, 'tm')  22.8 us
    all_gather x4, blocking collectives, body(): gains = lax.all_gather(fresh, 'grp', axis=2, tiled=True)  17.6 us
    all_gather x1, blocking collectives, body(): all_gains = lax.all_gather(gains, 'freq', axis=0, tiled=True)  13.4 us
  transfers between devices with their start and end apart: 3, of which 2 were waited for; matrix products, arithmetic and copies ran while one was open for 9% of the time, Pallas kernels for 0%

commit v1 on v0

--- a/solution.py
+++ b/solution.py
@@ -95,7 +95,9 @@
         real_imag = jnp.einsum("cij,cj->ci", vis_block[:, 0], along[:, 1], precision=highest)
         imag_real = jnp.einsum("cij,cj->ci", vis_block[:, 1], along[:, 0], precision=highest)
         update = jnp.stack([real_real - imag_imag, imag_real + real_imag], axis=1)
-        update = lax.psum(update, "tm")
+        update = update
+        for hop in (1, 2):
+            update = update + lax.ppermute(update, "tm", [(dev, dev ^ hop) for dev in range(4)])
         own_rows = lax.dynamic_slice_in_dim(gains, row_start, rows, 2)
         fresh = 0.5 * (own_rows + inputs_all * update / power[:, None, None])
         gains = lax.all_gather(fresh, "grp", axis=2, tiled=True)

time: 315 us -> 289 us (0.917)
  blocking collectives: 159 us -> 85.6 us
  waiting for transfers between devices: 79.2 us -> 118 us
  starting transfers between devices: 0.12 us -> 10.1 us
    all_gather x1, waiting for transfers between devices: 0.01 us -> 51.8 us  [body(): lax.all_gather(corr_half.reshape(split_shape), 'grp', axis=3, tiled=True)]
    all_to_all x1 -> x0, blocking collectives: 50.7 us -> none  [body(): lax.all_to_all(beam_source, 'freq', split_axis=0, concat_axis=2, tiled=True)]
    psum x4 -> x0, blocking collectives: 22.8 us -> none  [body(): update = lax.psum(update, 'tm')]
    all_gather x1, waiting for transfers between devices: 36.2 us -> 23.4 us  [body(): lax.all_gather(beam_half.reshape(split_shape), 'grp', axis=3, tiled=True)]
    reduce_scatter x1, waiting for transfers between devices: 42.9 us -> 33.2 us  [body(): lax.psum_scatter(partial_value, 'tm', scatter_dimension=3, tiled=True)]
    ppermute x0 -> x8, starting transfers between devices: none -> 5.3 us  [body(): lax.ppermute(update, 'tm', [(dev, dev ^ hop) for dev in range(4)])]
    all_to_all x0 -> x1, waiting for transfers between devices: none -> 4.82 us  [body(): lax.all_to_all(beam_source, 'freq', split_axis=0, concat_axis=2, tiled=True)]
    all_to_all x0 -> x1, starting transfers between devices: none -> 4.76 us  [body(): lax.all_to_all(beam_source, 'freq', split_axis=0, concat_axis=2, tiled=True)]
  transfers between devices with their start and end apart: 3 -> 12, of which waited for: 2 -> 9; matrix products, arithmetic and copies ran while one was open for 9% -> 11% of each run, Pallas kernels for 0% -> 0%
where the time goes in v1:
time: 289 us; the launch traced here: 288 us
  waiting for transfers between devices  118 us (41%)
  blocking collectives  85.6 us (30%)
  matrix products  24.5 us (8%)
  local copies, waits for them, and re-layouts  20.5 us (7%)
  between operations  17.4 us (6%)
  other arithmetic  12.2 us (4%)
  starting transfers between devices  10.1 us (3%)
    all_to_all x1, blocking collectives, body(): lax.all_to_all(corr_source, 'freq', split_axis=0, concat_axis=2, tiled=True)  54.4 us
    all_gather x1, waiting for transfers between devices, body(): lax.all_gather(corr_half.reshape(split_shape), 'grp', axis=3, tiled=True)  51.8 us
    reduce_scatter x1, waiting for transfers between devices, body(): lax.psum_scatter(partial_value, 'tm', scatter_dimension=3, tiled=True)  33.2 us
    all_gather x1, waiting for transfers between devices, body(): lax.all_gather(beam_half.reshape(split_shape), 'grp', axis=3, tiled=True)  23.4 us
    all_gather x4, blocking collectives, body(): gains = lax.all_gather(fresh, 'grp', axis=2, tiled=True)  18 us
    all_gather x1, blocking collectives, body(): all_gains = lax.all_gather(gains, 'freq', axis=0, tiled=True)  13.2 us
    dot_general x1, matrix products, body(): jnp.einsum('corit,crjt->coij', left, corr_volts, preferred_element_type=j...  6.09 us
  transfers between devices with their start and end apart: 12, of which 9 were waited for; matrix products, arithmetic and copies ran while one was open for 11% of the time, Pallas kernels for 0%

profile of v1, /device:TPU:0, one launch (start us, length us, event | category | flops | bytes accessed | tf_op | source)
XLA Modules:
  0.0 287.9 jit_solution(13810967356538818061)
XLA Ops:
  7.2 0.8 compare_select_fusion.1
  8.0 0.7 compare_and_fusion
  8.8 2.0 gather_fusion.2
  10.8 1.9 broadcast_select_fusion.1
  12.7 54.4 %all_to_all.30 = bf16[4,2,128,1024]{3,2,1,0:T(8,128)(2,1)} all-to-all(bf16[4,2,128,1024]{3,2,1,0:T(8,128)(2,1)S(1)} %broadcast_select_fusion.1), channel_id=1, replica_groups=mesh['freq'=4,'tm'=4,'grp'=2] {'freq'}, dimensions={0} | all-to-all | bytes 4194304 | tf_op jit(solution)/shard_map/all_to_all | solution.py:64
  67.2 0.6 copy-done.5
  67.8 3.5 %gather_fusion = s32[512]{0:T(512)S(1)} fusion(s32[512]{0:T(512)S(1)} %copy-done.1, s32[1024]{0:T(1024)S(1)} %pad_clamp_fusion.1), kind=kCustom, calls=%fused_computation.2 | custom fusion | bytes 6144 | tf_op jit(solution)/shard_map/jit(_take)/gather | solution.py:75
  71.5 51.8 %all-gather.3.cloned.1.call-done = bf16[1,2,4,256,1024]{4,3,1,2,0:T(8,128)(2,1)} async-done(((bf16[1,2,4,128,1024]{4,3,1,2,0:T(8,128)(2,1)}), bf16[1,2,4,256,1024]{4,3,1,2,0:T(8,128)(2,1)}) %all-gather.3.cloned.1.call-update) | async-done | bytes 4194320 | tf_op jit(solution)/shard_map/all_gather | solution.py:69
  123.3 2.6 copy.23
  126.7 1.8 copy-done.3
  129.6 6.1 %fusion.5 = f32[1,2,512,1024]{3,2,1,0:T(8,128)} fusion(bf16[2,1024,1024,1]{2,1,0,3:T(8,128)(2,1)S(1)} %bitcast.170, bf16[1,1,2,512,1024]{4,3,2,1,0:T(8,128)(2,1)S(1)} %maximum_bitcast_fusion.4, bf16[1,1,2,512,1024]{4,3,2,1,0:T(8,128)(2,1)S(1)} %fusion.80), kind=kOutput, calls=%fused_computation.11 | convolution fusion | flops 4298113024 | bytes 12582912 | tf_op jit(solution)/shard_map/corit,crjt->coij/dot_general | solution.py:83
  135.8 2.0 gather_fusion.3
  137.8 3.2 %broadcast_select_fusion = bf16[4,2,128,1024]{3,2,1,0:T(8,128)(2,1)} fusion(bf16[4,2,128,1024]{3,2,1,0:T(8,128)(2,1)} %gather_fusion.3, pred[4]{0:T(512)(128)(4,1)S(1)} %get-tuple-element.26), kind=kLoop, calls=%fused_computation.17 | loop fusion | flops 1048576 | bytes 4194308 | tf_op jit(solution)/shard_map/jit(_take)/select_n | solution.py:62
  141.0 4.8 %all-to-all-start.1 = ((bf16[4,2,128,1024]{3,2,1,0:T(8,128)(2,1)}), bf16[4,2,128,1024]{3,2,1,0:T(8,128)(2,1)}, u32[]{:S(2)}, u32[]{:S(2)}) async-start(bf16[4,2,128,1024]{3,2,1,0:T(8,128)(2,1)} %broadcast_select_fusion), calls=%async_computation.2 | async-start | bytes 4194304 | tf_op jit(solution)/shard_map/all_to_all | solution.py:65
  145.9 1.0 gather_fusion.1
  147.1 33.2 %reduce-scatter.2.cloned.1.call-done = f32[1,2,512,256]{3,2,1,0:T(8,128)} async-done(((f32[1,2,512,1024]{3,2,1,0:T(8,128)}), f32[1,2,512,256]{3,2,1,0:T(8,128)}) %reduce-scatter.2.cloned.1.call-update) | async-done | bytes 1048592 | tf_op jit(solution)/shard_map/reduce_scatter | solution.py:88
  180.3 1.7 fusion.29
  182.0 1.6 fusion.21
  183.6 1.6 fusion.22
  185.2 1.6 fusion.30
  186.9 0.6 multiply_reduce_fusion.3
  189.1 4.8 %all-to-all-done.1 = bf16[4,2,128,1024]{3,2,1,0:T(8,128)(2,1)} async-done(((bf16[4,2,128,1024]{3,2,1,0:T(8,128)(2,1)}), bf16[4,2,128,1024]{3,2,1,0:T(8,128)(2,1)}, u32[]{:S(2)}, u32[]{:S(2)}) %all-to-all-start.1) | async-done | bytes 2097184 | tf_op jit(solution)/shard_map/all_to_all | solution.py:65
  194.0 4.4 %all_gather.22 = f32[1,2,1024]{2,1,0:T(2,128)S(1)} all-gather(f32[1,2,512]{2,1,0:T(2,128)S(1)} %fusion.38), channel_id=1, replica_groups=mesh['freq'=4,'tm'=4,'grp'=2] {'grp'}, dimensions={2}, use_global_device_ids=true | all-gather | bytes 12288 | tf_op jit(solution)/shard_map/all_gather | solution.py:103
  198.9 0.6 fusion.19
  200.0 0.6 fusion.28
  200.7 1.1 collective-permute-done.2
  201.9 1.5 collective-permute-start.3
  203.4 0.6 multiply_reduce_fusion.2
  204.7 0.9 collective-permute-done.3
  205.6 4.8 %all_gather.23 = f32[1,2,1024]{2,1,0:T(2,128)S(1)} all-gather(f32[1,2,512]{2,1,0:T(2,128)S(1)} %fusion.39), channel_id=1, replica_groups=mesh['freq'=4,'tm'=4,'grp'=2] {'grp'}, dimensions={2}, use_global_device_ids=true | all-gather | bytes 12288 | tf_op jit(solution)/shard_map/all_gather | solution.py:103
  210.9 0.6 fusion.17
  212.0 0.6 fusion.26
  213.0 0.6 dynamic_slice.42
  214.2 1.5 collective-permute-start.5
  215.8 0.6 multiply_reduce_fusion.1
  217.0 0.9 collective-permute-done.5
  217.9 4.6 %all_gather.24 = f32[1,2,1024]{2,1,0:T(2,128)S(1)} all-gather(f32[1,2,512]{2,1,0:T(2,128)S(1)} %fusion.40), channel_id=1, replica_groups=mesh['freq'=4,'tm'=4,'grp'=2] {'grp'}, dimensions={2}, use_global_device_ids=true | all-gather | bytes 12288 | tf_op jit(solution)/shard_map/all_gather | solution.py:103
  224.8 1.0 fusion.32
  225.9 23.4 %all-gather.5.cloned.1.call-done = bf16[1,2,4,256,1024]{4,3,1,2,0:T(8,128)(2,1)} async-done(((bf16[1,2,4,128,1024]{4,3,1,2,0:T(8,128)(2,1)}), bf16[1,2,4,256,1024]{4,3,1,2,0:T(8,128)(2,1)}) %all-gather.5.cloned.1.call-update) | async-done | bytes 4194320 | tf_op jit(solution)/shard_map/all_gather | solution.py:70
  249.2 4.6 %copy.27 = bf16[1,2,4,256,1024]{4,3,2,1,0:T(8,128)(2,1)} copy(bf16[1,2,4,256,1024]{4,3,1,2,0:T(8,128)(2,1)} %all-gather.5.cloned.1.call-done) | data formatting | bytes 8388608 | tf_op jit(solution)/shard_map/all_gather | solution.py:70
  253.9 1.6 collective-permute-start.7
  255.4 0.6 multiply_reduce_fusion
  256.7 0.9 collective-permute-done.7
  257.6 4.4 %all_gather.25 = f32[1,2,1024]{2,1,0:T(2,128)S(1)} all-gather(f32[1,2,512]{2,1,0:T(2,128)S(1)} %fusion.41), channel_id=1, replica_groups=mesh['freq'=4,'tm'=4,'grp'=2] {'grp'}, dimensions={2}, use_global_device_ids=true | all-gather | bytes 12288 | tf_op jit(solution)/shard_map/all_gather | solution.py:103
  261.9 13.2 %all_gather.26 = f32[4,2,1024]{2,1,0:T(2,128)S(1)} all-gather(f32[1,2,1024]{2,1,0:T(2,128)S(1)} %all_gather.25), channel_id=1, replica_groups=mesh['freq'=4,'tm'=4,'grp'=2] {'freq'}, dimensions={0}, use_global_device_ids=true | all-gather | bytes 40960 | tf_op jit(solution)/shard_map/all_gather | solution.py:104
  275.1 0.8 fusion.33
  276.2 4.6 %fusion.8 = bf16[1,2,2,128,1024]{4,3,2,1,0:T(8,128)(2,1)} fusion(bf16[2,1,128,2,512]{4,2,3,1,0:T(8,128)(2,1)S(1)} %get-tuple-element.17, bf16[2,1,128,2,512]{4,2,3,1,0:T(8,128)(2,1)S(1)} %get-tuple-element.16, bf16[2,2,512,1024]{3,2,1,0:T(8,128)(2,1)} %bitcast.169, bf16[2,512]{1,0:T(2,128)(2,1)S(1)} %convert_element_type.50), kind=kOutput, calls=%fused_computation.19 | convolution fusion | flops 1076887552 | bytes 6293504 | tf_op jit(solution)/shard_map/cpobrq,crpqt->cpobt/dot_general | solution.py:116
  280.8 0.6 copy.47
  (88 shorter events, 9.1 us)
Async XLA Ops:
  7.2 1.6 copy-start
  7.2 116.1 %all-gather.3.cloned.1.call-start = ((), (), s32[]{:S(2)}) async-start(), calls=%async_computation.3 | async-start | bytes 6291456 | tf_op jit(solution)/shard_map/all_gather | solution.py:69
  67.1 0.7 copy-start.5
  67.1 0.7 copy-start.1
  67.1 113.2 %reduce-scatter.2.cloned.1.call-start = ((), (), s32[]{:S(2)}) async-start(), calls=%async_computation.4 | async-start | bytes 5242880 | tf_op jit(solution)/shard_map/reduce_scatter | solution.py:88
  126.3 2.2 copy-start.3
  141.0 4.8 %copy-start.7 = (f32[2,512]{1,0:T(2,128)S(1)}, f32[2,512]{1,0:T(2,128)}, u32[]{:S(2)}) copy-start(f32[2,512]{1,0:T(2,128)} %param.14) | copy-start | bytes 12292
  141.0 39.4 %copy-start.4 = (f32[1,2,1024]{2,1,0:T(2,128)S(1)}, f32[1,2,1024]{2,1,0:T(2,128)}, u32[]{:S(2)}) copy-start(f32[1,2,1024]{2,1,0:T(2,128)} %param.11) | copy-start | bytes 24580
  141.0 53.0 %all-to-all-start.1 = ((bf16[4,2,128,1024]{3,2,1,0:T(8,128)(2,1)}), bf16[4,2,128,1024]{3,2,1,0:T(8,128)(2,1)}, u32[]{:S(2)}, u32[]{:S(2)}) async-start(bf16[4,2,128,1024]{3,2,1,0:T(8,128)(2,1)} %broadcast_select_fusion), calls=%async_computation.2 | async-start | bytes 4194304 | tf_op jit(solution)/shard_map/all_to_all | solution.py:65
  145.8 42.7 %copy-start.9 = (s32[2,256]{1,0:T(2,128)S(1)}, s32[2,256]{1,0:T(2,128)}, u32[]{:S(2)}) copy-start(s32[2,256]{1,0:T(2,128)} %param.15) | copy-start | bytes 6148
  145.8 103.5 %all-gather.5.cloned.1.call-start = ((), (), s32[]{:S(2)}) async-start(), calls=%async_computation.5 | async-start | bytes 6291456 | tf_op jit(solution)/shard_map/all_gather | solution.py:70
  180.3 18.0 %copy-start.2 = (f32[1,2,512,256]{3,2,1,0:T(8,128)S(1)}, f32[1,2,512,256]{3,2,1,0:T(8,128)}, u32[]{:S(2)}) copy-start(f32[1,2,512,256]{3,2,1,0:T(8,128)} %reduce-scatter.2.cloned.1.call-done) | copy-start | bytes 3145732
  186.9 1.2 collective-permute-start
  188.1 5.9 %collective-permute-start.1 = (f32[1,2,512]{2,1,0:T(2,128)S(1)}, f32[1,2,512]{2,1,0:T(2,128)S(1)}, u32[]{:S(2)}, u32[]{:S(2)}) collective-permute-start(f32[1,2,512]{2,1,0:T(2,128)S(1)} %fusion.76), channel_id=1, source_target_pairs={{0,4},{2,6},{4,0},{6,2},{1,5},{3,7},{5,1},{7,3},{8,12},{10,14},{12... | collective-permute-start | bytes 12296 | tf_op jit(solution)/shard_map/ppermute | solution.py:100
  198.9 14.0 %copy-start.8 = (s32[4]{0:T(128)S(1)}, s32[4]{0:T(128)}, u32[]{:S(2)}) copy-start(s32[4]{0:T(128)} %param.17) | copy-start | bytes 52
  200.6 1.2 collective-permute-start.2
  201.9 3.7 %collective-permute-start.3 = (f32[1,2,512]{2,1,0:T(2,128)S(1)}, f32[1,2,512]{2,1,0:T(2,128)S(1)}, u32[]{:S(2)}, u32[]{:S(2)}) collective-permute-start(f32[1,2,512]{2,1,0:T(2,128)S(1)} %fusion.75), channel_id=1, source_target_pairs={{0,4},{2,6},{4,0},{6,2},{1,5},{3,7},{5,1},{7,3},{8,12},{10,14},{12... | collective-permute-start | bytes 12296 | tf_op jit(solution)/shard_map/ppermute | solution.py:100
  212.6 1.6 collective-permute-start.4
  214.2 3.7 %collective-permute-start.5 = (f32[1,2,512]{2,1,0:T(2,128)S(1)}, f32[1,2,512]{2,1,0:T(2,128)S(1)}, u32[]{:S(2)}, u32[]{:S(2)}) collective-permute-start(f32[1,2,512]{2,1,0:T(2,128)S(1)} %fusion.74), channel_id=1, source_target_pairs={{0,4},{2,6},{4,0},{6,2},{1,5},{3,7},{5,1},{7,3},{8,12},{10,14},{12... | collective-permute-start | bytes 12296 | tf_op jit(solution)/shard_map/ppermute | solution.py:100
  224.7 29.1 %collective-permute-start.6 = (f32[1,2,512]{2,1,0:T(2,128)S(1)}, f32[1,2,512]{2,1,0:T(2,128)S(1)}, u32[]{:S(2)}, u32[]{:S(2)}) collective-permute-start(f32[1,2,512]{2,1,0:T(2,128)S(1)} %pad_maximum_fusion.3), channel_id=1, source_target_pairs={{0,2},{2,0},{4,6},{6,4},{1,3},{3,1},{5,7},{7,5},{8,10},{10,8},{12,... | collective-permute-start | bytes 12296 | tf_op jit(solution)/shard_map/ppermute | solution.py:100
  225.9 49.2 %copy-start.6 = (s32[4]{0:T(128)S(1)}, s32[4]{0:T(128)}, u32[]{:S(2)}) copy-start(s32[4]{0:T(128)} %param.16) | copy-start | bytes 52
  253.9 3.7 %collective-permute-start.7 = (f32[1,2,512]{2,1,0:T(2,128)S(1)}, f32[1,2,512]{2,1,0:T(2,128)S(1)}, u32[]{:S(2)}, u32[]{:S(2)}) collective-permute-start(f32[1,2,512]{2,1,0:T(2,128)S(1)} %fusion.73), channel_id=1, source_target_pairs={{0,4},{2,6},{4,0},{6,2},{1,5},{3,7},{5,1},{7,3},{8,12},{10,14},{12... | collective-permute-start | bytes 12296 | tf_op jit(solution)/shard_map/ppermute | solution.py:100
Sparse Core Ops, SparseCore 0:
  67.3 55.9 all-gather.2
  135.9 44.4 reduce-scatter.1
  194.1 55.0 all-gather.4
